TPU v7x, 32 devices: a whole 2x2x4 slice. The times are simulated.
32 devices in a mesh: section: 8 (over y, x, core), rep: 4 (over z).
Axes of the slice: x: 2, y: 2, z: 4, core: 2. Of those that a mesh axis runs over, the one named last changes fastest.
Arguments:
- features: bfloat16 [16384, 128], P('section'), may hold values from -6 to 6
- order: int32 [16384], P('section'), may hold values from 0 to 2047, as said below
- tiles: bfloat16 [8, 4, 2, 96, 128, 128], P('section', 'rep'), may hold values from -0.125 to 0.125
- tile_rows: int32 [8, 4, 2, 96], P('section', 'rep'), may hold values from 0 to 15, as said below
- tile_cols: int32 [8, 4, 2, 96], P('section', 'rep'), may hold values from 0 to 15, as said below
- live: int32 [8, 4, 2], P('section', 'rep'), may hold values from 1 to 96, as said below
- weight: bfloat16 [128, 128], replicated, may hold values from -0.5 to 0.5
- cotangent: bfloat16 [16384, 128], P('section'), may hold values from -6 to 6
Outputs:
- hidden: bfloat16 [16384, 128], P('section')
- weight_grad: float32 [128, 128], replicated
- feature_grad: bfloat16 [16384, 128], P('section')
Inputs may be any that keep to these rules, and one draw needn't show every extreme that they name: `order`: within each panel of 2048 rows, a permutation of the local row numbers. For one section, replica and round, the 96 pairs (tile_rows, tile_cols) are distinct. `tile_cols`: block column within the panel j * 4 + r for replica r and round j. Some section, replica and round has all 96 slots live.
All inputs are finite; a program needn't handle non-finite values.
Results may differ from a plain program's by a relative error of at most 0.012.
Values may be sent and summed in bfloat16 or wider, within the bound.
No kernel may reach another device: no remote copies, remote signals or barrier semaphores. Data moves between devices by JAX's collectives and lax.ppermute only.
A program may use at most 192 MiB of HBM per device.

v0:
```python
import math
import jax
import jax.numpy as jnp
from jax import lax
from jax.sharding import PartitionSpec as P


def spread(value, axis, source):
    kept = jnp.where(lax.axis_index(axis) == source, value, 0).astype(value.dtype)
    return lax.psum(kept, axis)


def shards(features, order, tiles, tile_rows, tile_cols, live, weight, cotangent):
    rep_count = lax.axis_size("rep")
    section_count = lax.axis_size("section")
    rep_index = lax.axis_index("rep")
    section_index = lax.axis_index("section")
    panel_rows, width = features.shape
    block_rows = tiles.shape[-1]
    blocks = panel_rows // block_rows
    rounds = tiles.shape[2]
    slot_count = tiles.shape[3]
    own_tiles = tiles[0, 0]
    row_table = tile_rows[0, 0]
    col_table = tile_cols[0, 0]
    live_counts = live[0, 0]
    slot_ids = jnp.arange(slot_count, dtype=jnp.int32)
    block_ids = jnp.arange(blocks, dtype=jnp.int32)
    grad_scale = 1.0 / math.sqrt(panel_rows * section_count)
    reordered = jnp.take(features, order, axis=0)

    def forward_round(round_no, running):
        root = round_no * rep_count + rep_index
        panel = spread(reordered, "section", root)
        tile_set = lax.dynamic_index_in_dim(own_tiles, round_no, 0, keepdims=False)
        row_ids = lax.dynamic_index_in_dim(row_table, round_no, 0, keepdims=False)
        col_ids = lax.dynamic_index_in_dim(col_table, round_no, 0, keepdims=False)
        count_now = lax.dynamic_index_in_dim(live_counts, round_no, 0, keepdims=False)
        picked = jnp.take(panel.reshape(blocks, block_rows, width), col_ids, axis=0)
        products = jnp.einsum("kab,kbf->kaf", tile_set, picked, preferred_element_type=jnp.float32)
        select = (
            (row_ids[None, :] == block_ids[:, None]) & (slot_ids < count_now)[None, :]
        ).astype(jnp.float32)
        return running + jnp.einsum(
            "pk,kaf->paf", select, products, precision=lax.Precision.HIGHEST
        )

    partial_sum = lax.fori_loop(
        0, rounds, forward_round, jnp.zeros((blocks, block_rows, width), jnp.float32)
    )
    partial_sum = partial_sum.reshape(panel_rows, width)
    share_rows = panel_rows // rep_count
    row_share = lax.psum_scatter(partial_sum, "rep", scatter_dimension=0, tiled=True)
    co_share = lax.dynamic_slice_in_dim(cotangent, rep_index * share_rows, share_rows, 0)
    aggregated = row_share.astype(jnp.bfloat16)
    preact = jnp.dot(aggregated, weight, preferred_element_type=jnp.float32)
    out_rows = jax.nn.silu(preact).astype(jnp.bfloat16)
    sigmoid_part = jax.nn.sigmoid(preact)
    grad_pre = (
        co_share.astype(jnp.float32) * sigmoid_part * (1.0 + preact * (1.0 - sigmoid_part))
    ).astype(jnp.bfloat16)
    grad_part = jnp.einsum("nf,ng->fg", aggregated, grad_pre, preferred_element_type=jnp.float32)
    up_rows = jnp.einsum("ng,fg->nf", grad_pre, weight, preferred_element_type=jnp.float32).astype(
        jnp.bfloat16
    )
    hidden_share, grad_part, upstream_share = (out_rows, grad_part, up_rows)
    weight_grad = lax.psum(grad_part, ("section", "rep")) * grad_scale
    hidden, upstream = (
        lax.all_gather(hidden_share, "rep", axis=0, tiled=True),
        lax.all_gather(upstream_share, "rep", axis=0, tiled=True),
    )
    up_blocks = upstream.reshape(blocks, block_rows, width)
    picked_up = jnp.take(up_blocks, row_table.reshape(-1), axis=0).reshape(
        rounds, slot_count, block_rows, width
    )
    products_back = jnp.einsum(
        "jkab,jkaf->jkbf", own_tiles, picked_up, preferred_element_type=jnp.float32
    )
    alive_mask = slot_ids[None, None, :] < live_counts[:, None, None]
    select_back = ((col_table[:, None, :] == block_ids[None, :, None]) & alive_mask).astype(
        jnp.float32
    )
    contrib = jnp.einsum(
        "jpk,jkbf->jpbf", select_back, products_back, precision=lax.Precision.HIGHEST
    )
    contrib = lax.optimization_barrier(contrib.astype(jnp.bfloat16)).astype(jnp.float32)
    contrib = contrib.reshape(rounds, panel_rows, width)
    totals = lax.psum(contrib.astype(jnp.bfloat16), "section").astype(jnp.float32)
    own_panel = lax.dynamic_index_in_dim(
        totals, section_index // rep_count, 0, keepdims=False
    ).astype(jnp.bfloat16)
    grad_rows = spread(own_panel, "rep", section_index % rep_count)
    feature_grad = jnp.zeros_like(features).at[order].set(grad_rows)
    return (hidden, weight_grad, feature_grad)


def solution(mesh):
    placed = (
        P("section", None),
        P("section"),
        P("section", "rep", None, None, None, None),
        P("section", "rep", None, None),
        P("section", "rep", None, None),
        P("section", "rep", None),
        P(),
        P("section", None),
    )
    return jax.shard_map(
        shards,
        mesh=mesh,
        in_specs=placed,
        out_specs=(P("section", None), P(), P("section", None)),
        check_vma=False,
    )
```

profile of v0, /device:TPU:0, one launch (start us, length us, event | category | flops | bytes accessed | tf_op | source)
XLA Modules:
  0.0 487.0 jit_solution(13288153377587932532)
XLA Ops:
  9.5 6.2 %gather_fusion.1 = bf16[2048,128]{1,0:T(8,128)(2,1)S(1)} fusion(bf16[2048,128]{1,0:T(8,128)(2,1)S(1)} %copy-done, s32[2048]{0:T(1024)S(1)} %get-tuple-element.296), kind=kCustom, calls=%fused_computation.1 | custom fusion | bytes 1056768 | tf_op jit(solution)/shard_map/jit(_take)/gather | solution.py:30
  16.0 147.6 %while.16 = (s32[]{:T(128)}, f32[16,128,128]{2,0,1:T(8,128)S(1)}, s32[2,96]{1,0:T(2,128)}, s32[2]{0:T(128)}, bf16[2,96,128,128]{3,2,1,0:T(8,128)(2,1)}, /*index=...) while((s32[]{:T(128)}, f32[16,128,128]{2,0,1:T(8,128)S(1)}, ...), condition=%wide.region_2.3_spmd.clone, body=%wide.region_0.0_spmd.clone.sunk | while | flops 707269568 | bytes 31465112 | solution.py:48
  16.1 0.8 broadcast_select_fusion.3
  18.3 1.2 dynamic_slice.80
  20.9 57.2 %all-reduce.11.cloned.1.call-done = bf16[16,128,128]{2,1,0:T(8,128)(2,1)} async-done(((bf16[16,128,128]{2,1,0:T(8,128)(2,1)}), bf16[16,128,128]{2,1,0:T(8,128)(2,1)}) %all-reduce.11.cloned.1.call-update) | async-done | bytes 524304 | tf_op jit(solution)/shard_map/while/body/eval_jaxpr/psum | solution.py:10
  78.1 3.7 gather_fusion
  81.9 3.9 fusion.65
  85.8 5.7 %fusion.67 = f32[16,128,128]{2,0,1:T(8,128)S(1)} fusion(f32[96,128,128]{2,1,0:T(8,128)S(1)} %fusion.65, f32[16,128,128]{2,0,1:T(8,128)S(1)} %get-tuple-element.360, pred[]{:T(512)S(6)} %compare.6, s32[96]{0:T(128)S(1)} %fusion.66, pred[96]{0:T(512)(128)(4,1)S(1)} %iota_compare_fusion.5), kind=kOutput, calls=%fused_computation.14.clone.1 | convolution fusion | flops 302517248 | bytes 8389089 | tf_op jit(solution)/shard_map/while/body/eval_jaxpr/pk,kaf->paf/dot_general | solution.py:44
  91.6 0.8 broadcast_select_fusion.3
  93.8 1.2 dynamic_slice.80
  96.4 53.8 %all-reduce.11.cloned.1.call-done = bf16[16,128,128]{2,1,0:T(8,128)(2,1)} async-done(((bf16[16,128,128]{2,1,0:T(8,128)(2,1)}), bf16[16,128,128]{2,1,0:T(8,128)(2,1)}) %all-reduce.11.cloned.1.call-update) | async-done | bytes 524304 | tf_op jit(solution)/shard_map/while/body/eval_jaxpr/psum | solution.py:10
  150.2 3.7 gather_fusion
  154.0 3.9 fusion.65
  157.9 5.7 %fusion.67 = f32[16,128,128]{2,0,1:T(8,128)S(1)} fusion(f32[96,128,128]{2,1,0:T(8,128)S(1)} %fusion.65, f32[16,128,128]{2,0,1:T(8,128)S(1)} %get-tuple-element.360, pred[]{:T(512)S(6)} %compare.6, s32[96]{0:T(128)S(1)} %fusion.66, pred[96]{0:T(512)(128)(4,1)S(1)} %iota_compare_fusion.5), kind=kOutput, calls=%fused_computation.14.clone.1 | convolution fusion | flops 302517248 | bytes 8389089 | tf_op jit(solution)/shard_map/while/body/eval_jaxpr/pk,kaf->paf/dot_general | solution.py:44
  163.7 1.3 copy.11
  167.3 25.6 %reduce-scatter.2.cloned.1.call-done = f32[512,128]{1,0:T(8,128)} async-done(((f32[2048,128]{1,0:T(8,128)}), f32[512,128]{1,0:T(8,128)}) %reduce-scatter.2.cloned.1.call-update) | async-done | bytes 262160 | tf_op jit(solution)/shard_map/reduce_scatter | solution.py:53
  192.9 1.3 multiply_convert_fusion
  194.3 16.2 %all_gather.7 = bf16[2048,128]{1,0:T(8,128)(2,1)S(1)} all-gather(bf16[512,128]{1,0:T(8,128)(2,1)S(1)} %convolution_convert_fusion), channel_id=1, replica_groups=mesh['section'=8,'rep'=4] {'rep'}, dimensions={0}, use_global_device_ids=true | all-gather | bytes 655360 | tf_op jit(solution)/shard_map/all_gather | solution.py:70
  210.5 8.0 %gather_fusion.2 = bf16[192,128,128]{2,1,0:T(8,128)(2,1)} fusion(bf16[16,128,128]{2,1,0:T(8,128)(2,1)S(1)} %bitcast.60, s32[1024]{0:T(1024)S(1)} %pad_clamp_fusion.1), kind=kCustom, calls=%fused_computation.2 | custom fusion | bytes 12583680 | tf_op jit(solution)/shard_map/jit(_take)/gather | solution.py:73
  218.5 11.6 %fusion.26 = f32[2,96,128,128]{3,2,1,0:T(8,128)} fusion(bf16[2,96,128,128]{3,2,1,0:T(8,128)(2,1)} %bitcast.64, pred[2,96]{1,0:T(4,128)(4,1)S(1)} %compare_and_fusion.2, bf16[1,1,2,96,128,128]{5,4,3,2,1,0:T(8,128)(2,1)} %bitcast.62), kind=kOutput, calls=%fused_computation.34 | convolution fusion | flops 808452096 | bytes 25166016 | tf_op jit(solution)/shard_map/jkab,jkaf->jkbf/dot_general | solution.py:76
  230.1 12.8 %copy.14 = f32[2,96,128,128]{2,1,3,0:T(8,128)} copy(f32[2,96,128,128]{3,2,1,0:T(8,128)} %fusion.26) | data formatting | bytes 25165824 | tf_op jit(solution)/shard_map/jkab,jkaf->jkbf/dot_general | solution.py:76
  242.8 7.2 %fusion.30 = bf16[2,16,128,128]{3,1,2,0:T(8,128)(2,1)S(1)} fusion(f32[2,96,128,128]{2,1,3,0:T(8,128)} %copy.14, s32[2,96]{1,0:T(2,128)S(1)} %copy-done.3, pred[2,96]{1,0:T(4,128)(4,1)S(1)} %iota_compare_fusion.3), kind=kOutput, calls=%fused_computation.38 | convolution fusion | flops 604510208 | bytes 13632448 | tf_op jit(solution)/shard_map/jpk,jkbf->jpbf/dot_general | solution.py:83
  250.1 1.3 copy.12
  251.5 0.9 fusion.37
  252.5 53.3 %all-reduce.7.cloned.1.call-done = bf16[2,2048,128]{2,1,0:T(8,128)(2,1)} async-done(((bf16[2,2048,128]{2,1,0:T(8,128)(2,1)}), bf16[2,2048,128]{2,1,0:T(8,128)(2,1)}) %all-reduce.7.cloned.1.call-update) | async-done | bytes 1048592 | tf_op jit(solution)/shard_map/psum | solution.py:88
  305.8 1.9 fusion.34
  307.7 14.8 %all_gather.6 = bf16[2048,128]{1,0:T(8,128)(2,1)S(1)} all-gather(bf16[512,128]{1,0:T(8,128)(2,1)S(1)} %get-tuple-element.294), channel_id=1, replica_groups=mesh['section'=8,'rep'=4] {'rep'}, dimensions={0}, use_global_device_ids=true | all-gather | bytes 655360 | tf_op jit(solution)/shard_map/all_gather | solution.py:69
  322.5 106.7 %all-reduce.5.cloned.1.call-done = f32[128,128]{1,0:T(8,128)} async-done(((f32[128,128]{1,0:T(8,128)}), f32[128,128]{1,0:T(8,128)}) %all-reduce.5.cloned.1.call-update) | async-done | bytes 65552 | tf_op jit(solution)/shard_map/psum | solution.py:67
  429.3 1.5 broadcast_multiply_fusion
  430.7 41.1 %all-reduce.9.cloned.1.call-done = bf16[2048,128]{1,0:T(8,128)(2,1)} async-done(((bf16[2048,128]{1,0:T(8,128)(2,1)}), bf16[2048,128]{1,0:T(8,128)(2,1)}) %all-reduce.9.cloned.1.call-update) | async-done | bytes 524304 | tf_op jit(solution)/shard_map/psum | solution.py:10
  471.8 6.8 %scatter_custom_fusion = bf16[2048,128]{1,0:T(8,128)(2,1)} fusion(s32[2048]{0:T(1024)S(1)} %get-tuple-element.295, bf16[2048,128]{1,0:T(8,128)(2,1)} %all-reduce.9.cloned.1.call-done, bf16[]{:T(256)} %constant.190.clone.1), kind=kCustom, calls=%fused_computation.44 | custom fusion | bytes 524800 | tf_op jit(solution)/shard_map/scatter | solution.py:93
  478.7 0.8 copy.33
  (40 shorter events, 10.0 us)
Async XLA Ops:
  8.0 1.5 copy-start
  16.0 176.9 %copy-start.2 = (bf16[128,128]{1,0:T(8,128)(2,1)S(1)}, bf16[128,128]{1,0:T(8,128)(2,1)}, u32[]{:S(2)}) copy-start(bf16[128,128]{1,0:T(8,128)(2,1)} %param.16) | copy-start | bytes 98308
  16.0 62.1 %all-reduce.11.cloned.1.call-start = ((), (), s32[]{:S(2)}) async-start(), calls=%async_computation.5 | async-start | bytes 1048576 | tf_op jit(solution)/shard_map/while/body/eval_jaxpr/psum | solution.py:10
  91.5 58.7 %all-reduce.11.cloned.1.call-start = ((), (), s32[]{:S(2)}) async-start(), calls=%async_computation.5 | async-start | bytes 1048576 | tf_op jit(solution)/shard_map/while/body/eval_jaxpr/psum | solution.py:10
  163.6 29.2 %reduce-scatter.2.cloned.1.call-start = ((), (), s32[]{:S(2)}) async-start(), calls=%async_computation.1 | async-start | bytes 1310720 | tf_op jit(solution)/shard_map/reduce_scatter | solution.py:53
  165.0 140.7 %all-reduce.7.cloned.1.call-start = ((), (), s32[]{:S(2)}) async-start(), calls=%async_computation.3 | async-start | bytes 2097152 | tf_op jit(solution)/shard_map/psum | solution.py:88
  230.1 12.8 %copy-start.3 = (s32[2,96]{1,0:T(2,128)S(1)}, s32[2,96]{1,0:T(2,128)}, u32[]{:S(2)}) copy-start(s32[2,96]{1,0:T(2,128)} %get-tuple-element.411) | copy-start | bytes 2308
  242.8 8.7 %copy-start.1 = (f32[512,128]{1,0:T(8,128)S(1)}, f32[512,128]{1,0:T(8,128)}, u32[]{:S(2)}) copy-start(f32[512,128]{1,0:T(8,128)} %reduce-scatter.2.cloned.1.call-done) | copy-start | bytes 786436
  251.4 177.8 %all-reduce.5.cloned.1.call-start = ((), (), s32[]{:S(2)}) async-start(), calls=%async_computation.2 | async-start | bytes 131072 | tf_op jit(solution)/shard_map/psum | solution.py:67
  252.4 219.4 %all-reduce.9.cloned.1.call-start = ((), (), s32[]{:S(2)}) async-start(), calls=%async_computation.4 | async-start | bytes 1048576 | tf_op jit(solution)/shard_map/psum | solution.py:10
Sparse Core Ops, SparseCore 0:
  20.8 57.2 all-reduce.10
  96.3 53.8 all-reduce.10
Sparse Core Ops, SparseCore 1:
  166.4 26.4 reduce-scatter.1
  251.5 54.2 all-reduce.6
  312.7 116.5 all-reduce.4
  432.3 39.4 all-reduce.8
where the time goes:
time: 488 us; the launch traced here: 487 us
  waiting for transfers between devices  338 us (69%)
  local copies, waits for them, and re-layouts  49.3 us (10%)
  matrix products  40.4 us (8%)
  blocking collectives  31 us (6%)
  between operations  15.8 us (3%)
  other arithmetic  12.4 us (3%)
    psum x3, waiting for transfers between devices, spread(): return lax.psum(kept, axis)  152 us
    psum x1, waiting for transfers between devices, shards(): weight_grad = lax.psum(grad_part, ('section', 'rep')) * grad_scale  107 us
    psum x1, waiting for transfers between devices, shards(): lax.psum(contrib.astype(jnp.bfloat16), 'section').astype(jnp.float32)  53.3 us
    reduce_scatter x1, waiting for transfers between devices, shards(): lax.psum_scatter(partial_sum, 'rep', scatter_dimension=0, tiled=True)  25.6 us
    all_gather x1, blocking collectives, shards(): lax.all_gather(upstream_share, 'rep', axis=0, tiled=True)  16.2 us
    all_gather x1, blocking collectives, shards(): lax.all_gather(hidden_share, 'rep', axis=0, tiled=True)  14.8 us
    dot_general x1, local copies, waits for them, and re-layouts, shards(): jnp.einsum('jkab,jkaf->jkbf', own_tiles, picked_up, preferred_element_typ...  12.8 us
    dot_general x1, matrix products, shards(): jnp.einsum('jkab,jkaf->jkbf', own_tiles, picked_up, preferred_element_typ...  11.6 us
  transfers between devices with their start and end apart: 6, of which 6 were waited for; matrix products, arithmetic and copies ran while one was open for 3% of the time, Pallas kernels for 0%

commit v1 on v0

--- a/solution.py
+++ b/solution.py
@@ -64,7 +64,7 @@
         jnp.bfloat16
     )
     hidden_share, grad_part, upstream_share = (out_rows, grad_part, up_rows)
-    weight_grad = lax.psum(grad_part, ("section", "rep")) * grad_scale
+    weight_grad = lax.psum(lax.psum(grad_part, "rep"), "section") * grad_scale
     hidden, upstream = (
         lax.all_gather(hidden_share, "rep", axis=0, tiled=True),
         lax.all_gather(upstream_share, "rep", axis=0, tiled=True),

time: 488 us -> 446 us (0.914)
  waiting for transfers between devices: 338 us -> 296 us
    psum x1 -> x2, waiting for transfers between devices: 107 us -> 61.2 us  [shards(): weight_grad = lax.psum(lax.psum(grad_part, 'rep'), 'section') * grad_scale]
    psum x1, waiting for transfers between devices: 53.3 us -> 58.6 us  [shards(): lax.psum(contrib.astype(jnp.bfloat16), 'section').astype(jnp.float32)]
  transfers between devices with their start and end apart: 6 -> 7, of which waited for: 6 -> 7; matrix products, arithmetic and copies ran while one was open for 3% -> 5% of each run, Pallas kernels for 0% -> 0%
where the time goes in v1:
time: 446 us; the launch traced here: 445 us
  waiting for transfers between devices  296 us (66%)
  local copies, waits for them, and re-layouts  49.3 us (11%)
  matrix products  40.3 us (9%)
  blocking collectives  30.9 us (7%)
  between operations  15.8 us (4%)
  other arithmetic  12.4 us (3%)
    psum x3, waiting for transfers between devices, spread(): return lax.psum(kept, axis)  151 us
    psum x2, waiting for transfers between devices, shards(): weight_grad = lax.psum(lax.psum(grad_part, 'rep'), 'section') * grad_scale  61.2 us
    psum x1, waiting for transfers between devices, shards(): lax.psum(contrib.astype(jnp.bfloat16), 'section').astype(jnp.float32)  58.6 us
    reduce_scatter x1, waiting for transfers between devices, shards(): lax.psum_scatter(partial_sum, 'rep', scatter_dimension=0, tiled=True)  25.6 us
    all_gather x1, blocking collectives, shards(): lax.all_gather(upstream_share, 'rep', axis=0, tiled=True)  16.2 us
    all_gather x1, blocking collectives, shards(): lax.all_gather(hidden_share, 'rep', axis=0, tiled=True)  14.7 us
    dot_general x1, local copies, waits for them, and re-layouts, shards(): jnp.einsum('jkab,jkaf->jkbf', own_tiles, picked_up, preferred_element_typ...  12.8 us
    dot_general x1, matrix products, shards(): jnp.einsum('jkab,jkaf->jkbf', own_tiles, picked_up, preferred_element_typ...  11.5 us
  transfers between devices with their start and end apart: 7, of which 7 were waited for; matrix products, arithmetic and copies ran while one was open for 5% of the time, Pallas kernels for 0%

profile of v1, /device:TPU:0, one launch (start us, length us, event | category | flops | bytes accessed | tf_op | source)
XLA Modules:
  0.0 445.5 jit_solution(15518854962776417311)
XLA Ops:
  9.5 6.2 %gather_fusion.1 = bf16[2048,128]{1,0:T(8,128)(2,1)S(1)} fusion(bf16[2048,128]{1,0:T(8,128)(2,1)S(1)} %copy-done, s32[2048]{0:T(1024)S(1)} %get-tuple-element.296), kind=kCustom, calls=%fused_computation.1 | custom fusion | bytes 1056768 | tf_op jit(solution)/shard_map/jit(_take)/gather | solution.py:30
  16.0 147.6 %while.16 = (s32[]{:T(128)}, f32[16,128,128]{2,0,1:T(8,128)S(1)}, s32[2,96]{1,0:T(2,128)}, s32[2]{0:T(128)}, bf16[2,96,128,128]{3,2,1,0:T(8,128)(2,1)}, /*index=...) while((s32[]{:T(128)}, f32[16,128,128]{2,0,1:T(8,128)S(1)}, ...), condition=%wide.region_2.3_spmd.clone, body=%wide.region_0.0_spmd.clone.sunk | while | flops 707269568 | bytes 31465112 | solution.py:48
  16.1 0.8 broadcast_select_fusion.3
  18.3 1.2 dynamic_slice.80
  20.9 57.2 %all-reduce.14.cloned.1.call-done = bf16[16,128,128]{2,1,0:T(8,128)(2,1)} async-done(((bf16[16,128,128]{2,1,0:T(8,128)(2,1)}), bf16[16,128,128]{2,1,0:T(8,128)(2,1)}) %all-reduce.14.cloned.1.call-update) | async-done | bytes 524304 | tf_op jit(solution)/shard_map/while/body/eval_jaxpr/psum | solution.py:10
  78.1 3.7 gather_fusion
  81.9 3.9 fusion.65
  85.8 5.7 %fusion.67 = f32[16,128,128]{2,0,1:T(8,128)S(1)} fusion(f32[96,128,128]{2,1,0:T(8,128)S(1)} %fusion.65, f32[16,128,128]{2,0,1:T(8,128)S(1)} %get-tuple-element.360, pred[]{:T(512)S(6)} %compare.6, s32[96]{0:T(128)S(1)} %fusion.66, pred[96]{0:T(512)(128)(4,1)S(1)} %iota_compare_fusion.5), kind=kOutput, calls=%fused_computation.14.clone.1 | convolution fusion | flops 302517248 | bytes 8389089 | tf_op jit(solution)/shard_map/while/body/eval_jaxpr/pk,kaf->paf/dot_general | solution.py:44
  91.6 0.8 broadcast_select_fusion.3
  93.8 1.2 dynamic_slice.80
  96.4 53.8 %all-reduce.14.cloned.1.call-done = bf16[16,128,128]{2,1,0:T(8,128)(2,1)} async-done(((bf16[16,128,128]{2,1,0:T(8,128)(2,1)}), bf16[16,128,128]{2,1,0:T(8,128)(2,1)}) %all-reduce.14.cloned.1.call-update) | async-done | bytes 524304 | tf_op jit(solution)/shard_map/while/body/eval_jaxpr/psum | solution.py:10
  150.2 3.7 gather_fusion
  154.0 3.9 fusion.65
  157.9 5.7 %fusion.67 = f32[16,128,128]{2,0,1:T(8,128)S(1)} fusion(f32[96,128,128]{2,1,0:T(8,128)S(1)} %fusion.65, f32[16,128,128]{2,0,1:T(8,128)S(1)} %get-tuple-element.360, pred[]{:T(512)S(6)} %compare.6, s32[96]{0:T(128)S(1)} %fusion.66, pred[96]{0:T(512)(128)(4,1)S(1)} %iota_compare_fusion.5), kind=kOutput, calls=%fused_computation.14.clone.1 | convolution fusion | flops 302517248 | bytes 8389089 | tf_op jit(solution)/shard_map/while/body/eval_jaxpr/pk,kaf->paf/dot_general | solution.py:44
  163.7 1.3 copy.11
  167.3 25.6 %reduce-scatter.2.cloned.1.call-done = f32[512,128]{1,0:T(8,128)} async-done(((f32[2048,128]{1,0:T(8,128)}), f32[512,128]{1,0:T(8,128)}) %reduce-scatter.2.cloned.1.call-update) | async-done | bytes 262160 | tf_op jit(solution)/shard_map/reduce_scatter | solution.py:53
  192.9 1.3 multiply_convert_fusion
  194.3 16.2 %all_gather.7 = bf16[2048,128]{1,0:T(8,128)(2,1)S(1)} all-gather(bf16[512,128]{1,0:T(8,128)(2,1)S(1)} %convolution_convert_fusion), channel_id=1, replica_groups=mesh['section'=8,'rep'=4] {'rep'}, dimensions={0}, use_global_device_ids=true | all-gather | bytes 655360 | tf_op jit(solution)/shard_map/all_gather | solution.py:70
  210.5 8.0 %gather_fusion.2 = bf16[192,128,128]{2,1,0:T(8,128)(2,1)} fusion(bf16[16,128,128]{2,1,0:T(8,128)(2,1)S(1)} %bitcast.60, s32[1024]{0:T(1024)S(1)} %pad_clamp_fusion.1), kind=kCustom, calls=%fused_computation.2 | custom fusion | bytes 12583680 | tf_op jit(solution)/shard_map/jit(_take)/gather | solution.py:73
  218.6 11.5 %fusion.26 = f32[2,96,128,128]{3,2,1,0:T(8,128)} fusion(bf16[2,96,128,128]{3,2,1,0:T(8,128)(2,1)} %bitcast.64, pred[2,96]{1,0:T(4,128)(4,1)S(1)} %compare_and_fusion.2, bf16[1,1,2,96,128,128]{5,4,3,2,1,0:T(8,128)(2,1)} %bitcast.62), kind=kOutput, calls=%fused_computation.34 | convolution fusion | flops 808452096 | bytes 25166016 | tf_op jit(solution)/shard_map/jkab,jkaf->jkbf/dot_general | solution.py:76
  230.1 12.8 %copy.14 = f32[2,96,128,128]{2,1,3,0:T(8,128)} copy(f32[2,96,128,128]{3,2,1,0:T(8,128)} %fusion.26) | data formatting | bytes 25165824 | tf_op jit(solution)/shard_map/jkab,jkaf->jkbf/dot_general | solution.py:76
  242.9 0.9 fusion.37
  243.8 7.2 %fusion.30 = bf16[2,16,128,128]{3,1,2,0:T(8,128)(2,1)S(1)} fusion(f32[2,96,128,128]{2,1,3,0:T(8,128)} %copy.14, s32[2,96]{1,0:T(2,128)S(1)} %copy-done.3, pred[2,96]{1,0:T(4,128)(4,1)S(1)} %iota_compare_fusion.3), kind=kOutput, calls=%fused_computation.38 | convolution fusion | flops 604510208 | bytes 13632448 | tf_op jit(solution)/shard_map/jpk,jkbf->jpbf/dot_general | solution.py:83
  251.0 1.3 copy.12
  252.4 23.4 %all-reduce.6.cloned.1.call-done = f32[128,128]{1,0:T(8,128)} async-done(((f32[128,128]{1,0:T(8,128)}), f32[128,128]{1,0:T(8,128)}) %all-reduce.6.cloned.1.call-update) | async-done | bytes 65552 | tf_op jit(solution)/shard_map/psum | solution.py:67
  275.9 58.6 %all-reduce.10.cloned.1.call-done = bf16[2,2048,128]{2,1,0:T(8,128)(2,1)} async-done(((bf16[2,2048,128]{2,1,0:T(8,128)(2,1)}), bf16[2,2048,128]{2,1,0:T(8,128)(2,1)}) %all-reduce.10.cloned.1.call-update) | async-done | bytes 1048592 | tf_op jit(solution)/shard_map/psum | solution.py:88
  334.5 1.9 fusion.34
  336.5 14.7 %all_gather.6 = bf16[2048,128]{1,0:T(8,128)(2,1)S(1)} all-gather(bf16[512,128]{1,0:T(8,128)(2,1)S(1)} %get-tuple-element.294), channel_id=1, replica_groups=mesh['section'=8,'rep'=4] {'rep'}, dimensions={0}, use_global_device_ids=true | all-gather | bytes 655360 | tf_op jit(solution)/shard_map/all_gather | solution.py:69
  351.2 37.8 %all-reduce.8.cloned.1.call-done = f32[128,128]{1,0:T(8,128)} async-done(((f32[128,128]{1,0:T(8,128)}), f32[128,128]{1,0:T(8,128)}) %all-reduce.8.cloned.1.call-update) | async-done | bytes 65552 | tf_op jit(solution)/shard_map/psum | solution.py:67
  389.0 1.5 broadcast_multiply_fusion
  390.5 39.7 %all-reduce.12.cloned.1.call-done = bf16[2048,128]{1,0:T(8,128)(2,1)} async-done(((bf16[2048,128]{1,0:T(8,128)(2,1)}), bf16[2048,128]{1,0:T(8,128)(2,1)}) %all-reduce.12.cloned.1.call-update) | async-done | bytes 524304 | tf_op jit(solution)/shard_map/psum | solution.py:10
  430.3 6.8 %scatter_custom_fusion = bf16[2048,128]{1,0:T(8,128)(2,1)} fusion(s32[2048]{0:T(1024)S(1)} %get-tuple-element.295, bf16[2048,128]{1,0:T(8,128)(2,1)} %all-reduce.12.cloned.1.call-done, bf16[]{:T(256)} %constant.190.clone.1), kind=kCustom, calls=%fused_computation.44 | custom fusion | bytes 524800 | tf_op jit(solution)/shard_map/scatter | solution.py:93
  (43 shorter events, 10.9 us)
Async XLA Ops:
  8.0 1.5 copy-start
  16.0 176.9 %copy-start.2 = (bf16[128,128]{1,0:T(8,128)(2,1)S(1)}, bf16[128,128]{1,0:T(8,128)(2,1)}, u32[]{:S(2)}) copy-start(bf16[128,128]{1,0:T(8,128)(2,1)} %param.16) | copy-start | bytes 98308
  16.0 62.1 %all-reduce.14.cloned.1.call-start = ((), (), s32[]{:S(2)}) async-start(), calls=%async_computation.6 | async-start | bytes 1048576 | tf_op jit(solution)/shard_map/while/body/eval_jaxpr/psum | solution.py:10
  91.5 58.7 %all-reduce.14.cloned.1.call-start = ((), (), s32[]{:S(2)}) async-start(), calls=%async_computation.6 | async-start | bytes 1048576 | tf_op jit(solution)/shard_map/while/body/eval_jaxpr/psum | solution.py:10
  163.6 29.2 %reduce-scatter.2.cloned.1.call-start = ((), (), s32[]{:S(2)}) async-start(), calls=%async_computation.1 | async-start | bytes 1310720 | tf_op jit(solution)/shard_map/reduce_scatter | solution.py:53
  165.0 110.8 %all-reduce.6.cloned.1.call-start = ((), (), s32[]{:S(2)}) async-start(), calls=%async_computation.2 | async-start | bytes 131072 | tf_op jit(solution)/shard_map/psum | solution.py:67
  230.1 12.8 %copy-start.1 = (f32[512,128]{1,0:T(8,128)S(1)}, f32[512,128]{1,0:T(8,128)}, u32[]{:S(2)}) copy-start(f32[512,128]{1,0:T(8,128)} %reduce-scatter.2.cloned.1.call-done) | copy-start | bytes 786436
  230.1 13.7 %copy-start.3 = (s32[2,96]{1,0:T(2,128)S(1)}, s32[2,96]{1,0:T(2,128)}, u32[]{:S(2)}) copy-start(s32[2,96]{1,0:T(2,128)} %get-tuple-element.415) | copy-start | bytes 2308
  243.7 90.8 %all-reduce.10.cloned.1.call-start = ((), (), s32[]{:S(2)}) async-start(), calls=%async_computation.4 | async-start | bytes 2097152 | tf_op jit(solution)/shard_map/psum | solution.py:88
  252.4 136.7 %all-reduce.8.cloned.1.call-start = ((), (), s32[]{:S(2)}) async-start(), calls=%async_computation.3 | async-start | bytes 131072 | tf_op jit(solution)/shard_map/psum | solution.py:67
  275.8 154.4 %all-reduce.12.cloned.1.call-start = ((), (), s32[]{:S(2)}) async-start(), calls=%async_computation.5 | async-start | bytes 1048576 | tf_op jit(solution)/shard_map/psum | solution.py:10
Sparse Core Ops, SparseCore 0:
  20.8 57.2 all-reduce.13
  96.3 53.8 all-reduce.13
Sparse Core Ops, SparseCore 1:
  166.4 26.4 reduce-scatter.1
  243.8 31.9 all-reduce.5
  278.8 55.6 all-reduce.9
  337.6 51.4 all-reduce.7
  392.1 38.1 all-reduce.11
